TPU v7x, 32 devices: a whole 2x2x4 slice. The times are simulated.
32 devices in a mesh: gz: 4 (over z), gx: 2 (over x), gy: 4 (over y, core).
Axes of the slice: x: 2, y: 2, z: 4, core: 2. Of those that a mesh axis runs over, the one named last changes fastest.
Arguments:
- density: float32 [128, 256, 512], P('gx', 'gy', 'gz'), may hold values from 0.01 to 1
- design_mask: int32 [128, 256, 512], P('gx', 'gy', 'gz'), may hold values from 0 to 2
- energy: bfloat16 [4, 128, 256, 512], P(None, 'gx', 'gy', 'gz'), may hold values from 0.099609375 to 3
- decay: float32 [4, 512], P(None, 'gz'), may hold values from 0.3 to 1
- case_index: int32 [4], replicated, may hold values from 0 to 15
- case_weight: float32 [16], replicated, may hold values from 0.2 to 1
Outputs:
- sensitivity: float32 [128, 256, 512], P('gx', 'gy', 'gz')
- compliance: float32 [4], replicated
All inputs are finite; a program needn't handle non-finite values.
Results may differ from a plain program's by a relative error of at most 0.0006.
Values may be sent and summed in bfloat16 or wider, within the bound.
No kernel may reach another device: no remote copies, remote signals or barrier semaphores. Data moves between devices by JAX's collectives and lax.ppermute only.
A program may use at most 128 MiB of HBM per device.

v0:
```python
import jax
import jax.numpy as jnp
from jax import lax
from jax.sharding import PartitionSpec as P

LOADS = 16
RADIUS = 3


def entering_2(value, axis, join, neutral, backward):
    count, mine = (lax.axis_size(axis), lax.axis_index(axis))
    pieces = jax.tree.map(lambda part: lax.all_gather(part, axis), value)
    if backward:
        pieces = jax.tree.map(lambda part: part[::-1], pieces)
        mine = count - 1 - mine
    total = jax.tree.map(
        lambda part, zero: jnp.full_like(part, 0) + jnp.asarray(zero, part.dtype), value, neutral
    )

    def step(position, total):
        longer = join(total, jax.tree.map(lambda part: part[position], pieces))
        return jax.tree.map(lambda new, old: jnp.where(position < mine, new, old), longer, total)

    return lax.fori_loop(0, count - 1, step, total)


def with_halo(shard, sides, width):
    for axis, dim in sides:
        devices, length = (lax.axis_size(axis), shard.shape[dim])
        up = [(i, (i + 1) % devices) for i in range(devices - 1)]
        down = [(j, i) for i, j in up]
        last = lax.slice_in_dim(shard, length - width, length, axis=dim)
        initial = lax.slice_in_dim(shard, 0, width, axis=dim)
        before = lax.ppermute(last, axis, up)
        after = lax.ppermute(initial, axis, down)
        shard = jnp.concatenate([before, shard, after], axis=dim)
    return shard


def kernel_taps():
    offsets = jnp.arange(-RADIUS, RADIUS + 1).astype(jnp.float32)
    raw_taps = jnp.exp(-2.0 * offsets * offsets / (RADIUS * RADIUS))
    return raw_taps / jnp.sum(raw_taps)


def planar_filter(padded):
    width_x = padded.shape[1] - 2 * RADIUS
    width_y = padded.shape[2] - 2 * RADIUS
    taps = kernel_taps()
    along_x = taps[0] * padded[:, 0:width_x]
    for offset in range(1, 2 * RADIUS + 1):
        along_x = along_x + taps[offset] * padded[:, offset : offset + width_x]
    along_y = taps[0] * along_x[:, :, 0:width_y]
    for offset in range(1, 2 * RADIUS + 1):
        along_y = along_y + taps[offset] * along_x[:, :, offset : offset + width_y]
    return along_y


def solid_density(density, design_mask):
    return jnp.where(design_mask == 1, 0.001, jnp.where(design_mask == 2, 1.0, density))


def chain_maps(earlier, later):
    return (earlier[0] * later[0], later[0] * earlier[1] + later[1])


def slab_smooth(field, decay):
    depth = decay.shape[1]
    logs = jnp.log(decay)
    row_index = jnp.arange(depth)[:, None]
    col_index = jnp.arange(depth)[None, :]
    below_mask = (row_index >= col_index)[None]
    above_mask = (row_index <= col_index)[None]
    keep_in = (1.0 - decay)[:, None, :]
    upward = jnp.cumsum(logs, axis=1)
    spread = upward[:, :, None] - upward[:, None, :]
    forward_map = jnp.where(below_mask, jnp.exp(jnp.where(below_mask, spread, 0.0)), 0.0) * keep_in
    local_forward = jnp.einsum(
        "cxyj,cij->cxyi", field, forward_map, precision=lax.Precision.HIGHEST
    )
    leading = jnp.exp(upward)
    ones_part = jnp.ones((field.shape[0], 1, 1), jnp.float32)
    zero_part = jnp.zeros(field.shape[:3], jnp.float32)
    _, entering = entering_2(
        (leading[:, -1][:, None, None], local_forward[..., -1]),
        "gz",
        chain_maps,
        (ones_part, zero_part),
        False,
    )
    forward = local_forward + leading[:, None, None, :] * entering[..., None]
    remain = jnp.cumsum(logs[:, ::-1], axis=1)[:, ::-1]
    spread_back = remain[:, :, None] - remain[:, None, :]
    backward_map = (
        jnp.where(above_mask, jnp.exp(jnp.where(above_mask, spread_back, 0.0)), 0.0) * keep_in
    )
    local_backward = jnp.einsum(
        "cxyj,cij->cxyi", forward, backward_map, precision=lax.Precision.HIGHEST
    )
    trailing = jnp.exp(remain)
    _, from_above = entering_2(
        (trailing[:, 0][:, None, None], local_backward[..., 0]),
        "gz",
        chain_maps,
        (ones_part, zero_part),
        True,
    )
    return local_backward + trailing[:, None, None, :] * from_above[..., None]


def shards(density, design_mask, energy, decay, case_index, case_weight):
    dense = solid_density(density, design_mask)
    energy_wide = energy.astype(jnp.float32)
    source = -3.0 * (dense**3)[None] * energy_wide
    along_z = slab_smooth(source, decay)
    padded = with_halo(along_z.astype(jnp.bfloat16), (("gx", 1), ("gy", 2)), RADIUS).astype(
        along_z.dtype
    )
    smooth = planar_filter(padded)
    filtered = smooth / jnp.maximum(dense, 0.1)[None]
    selector = (case_index[:, None] == jnp.arange(LOADS)[None, :]).astype(jnp.float32)
    weights = jnp.sum(selector * case_weight[None, :], axis=1)
    combined = jnp.sum(weights[:, None, None, None] * filtered, axis=0)
    sensitivity = jnp.where(design_mask == 0, combined, 0.0).astype(jnp.float32)
    partial_sums = jnp.sum((dense**3)[None] * energy_wide, axis=(1, 2, 3))
    totals = lax.psum(partial_sums, ("gz", "gx", "gy"))
    all_cells = (
        density.shape[0]
        * density.shape[1]
        * density.shape[2]
        * lax.axis_size("gz")
        * lax.axis_size("gx")
        * lax.axis_size("gy")
    )
    return (sensitivity, totals / all_cells)


def solution(mesh):
    placed = (
        P("gx", "gy", "gz"),
        P("gx", "gy", "gz"),
        P(None, "gx", "gy", "gz"),
        P(None, "gz"),
        P(),
        P(),
    )
    return jax.shard_map(
        shards, mesh=mesh, in_specs=placed, out_specs=(P("gx", "gy", "gz"), P()), check_vma=False
    )
```

profile of v0, /device:TPU:1, one launch (start us, length us, event | category | flops | bytes accessed | tf_op | source)
XLA Modules:
  0.0 231.6 jit_solution(8170152929128144087)
XLA Ops:
  4.9 10.7 %all-reduce.2 = (f32[16]{0:T(128)S(1)}, f32[16]{0:T(128)S(1)}) all-reduce(f32[16]{0:T(128)S(1)} %dynamic-update-slice, f32[16]{0:T(128)S(1)} %dynamic-update-slice.1), channel_id=2, replica_groups=mesh['gz'=4,'gx'=2,'gy'=4] {'gz'}, use_global_device_ids=true, to_apply=%add | all-reduce | flops 32 | bytes 256
  15.8 4.5 %broadcast_multiply_fusion = (f32[64,64,128]{2,1,0:T(8,128)S(1)}, f32[64,64,128]{2,1,0:T(8,128)}, f32[64,64,128]{2,1,0:T(8,128)S(1)}) fusion(f32[64,64,128]{2,1,0:T(8,128)} %param.10, s32[64,64,128]{2,1,0:T(8,128)} %param.11), kind=kLoop, calls=%fused_computation.51 | loop fusion | flops 4194304 | bytes 10485760 | tf_op jit(solution)/shard_map/mul | solution.py:114
  20.3 8.6 %fusion.8 = f32[4,64,64,128]{3,2,1,0:T(8,128)S(1)} fusion(bf16[4,64,64,128]{3,2,1,0:T(8,128)(2,1)S(1)} %copy-done.2, f32[64,64,128]{2,1,0:T(8,128)S(1)} %get-tuple-element.290, f32[4,128]{1,0:T(4,128)S(1)} %get-tuple-element.298, f32[4,128]{1,0:T(4,128)S(1)} %reduce_window_sum.17, pred[128,128]{1,0:T(8,128)(4,1)S(1)} %iota_compare_fusion.1), kind=kOutput, calls=%fused_computation.21 | convolution fusion | flops 3225681920 | bytes 14700544 | tf_op jit(solution)/shard_map/cxyj,cij->cxyi/dot_general | solution.py:78
  28.9 3.2 %copy-done = f32[4,64,64,128]{3,2,1,0:T(8,128)} copy-done((f32[4,64,64,128]{3,2,1,0:T(8,128)}, f32[4,64,64,128]{3,2,1,0:T(8,128)S(1)}, u32[]{:S(2)}) %copy-start) | copy-done | bytes 8388632
  32.1 5.4 %slice.123 = f32[4,64,64,1]{3,2,1,0:T(8,128)} slice(f32[4,64,64,128]{3,2,1,0:T(8,128)S(1)} %fusion.8), slice={[0:4], [0:64], [0:64], [127:128]} | slice | bytes 131072 | tf_op jit(solution)/shard_map/slice | solution.py:85
  37.6 5.4 %copy.16 = f32[4,64,64,1]{2,1,3,0:T(8,128)S(1)} copy(f32[4,64,64,1]{3,2,1,0:T(8,128)} %slice.123) | data formatting | bytes 131072 | tf_op jit(solution)/shard_map/slice | solution.py:85
  43.0 12.8 %all-gather.1 = f32[16,64,64,1]{2,1,3,0:T(8,128)S(1)} all-gather(f32[4,64,64,1]{2,1,3,0:T(8,128)S(1)} %copy.16), channel_id=3, replica_groups=mesh['gz'=4,'gx'=2,'gy'=4] {'gz'}, dimensions={0}, use_global_device_ids=true | all-gather | bytes 327680 | tf_op jit(solution)/shard_map/all_gather | solution.py:12
  56.1 11.1 %fusion.18 = f32[4,64,64,128]{3,2,1,0:T(8,128)} fusion(f32[4,64,64,128]{3,2,1,0:T(8,128)} %copy-done, f32[4,64,64]{2,1,0:T(8,128)S(1)} %get-tuple-element.190, f32[4,128]{1,0:T(4,128)S(1)} %exp.23, f32[4,128]{1,0:T(4,128)S(1)} %rev.13, f32[4,128]{1,0:T(4,128)S(1)} %get-tuple-element.298, pred[128,128]{1,0:T(8,128)(4,1)S(1)} %iota_compare_fusion), kind=kOutput, calls=%fused_computation.39 | convolution fusion | flops 3225681920 | bytes 16865280 | tf_op jit(solution)/shard_map/cxyj,cij->cxyi/dot_general | solution.py:97
  67.2 5.4 %copy.18 = f32[4,64,64,1]{2,1,3,0:T(8,128)S(1)} copy(f32[4,64,64,1]{3,2,1,0:T(8,128)} %bitcast.43) | data formatting | bytes 131072 | tf_op jit(solution)/shard_map/slice | solution.py:102
  72.6 13.0 %all-gather.3 = f32[16,64,64,1]{2,1,3,0:T(8,128)S(1)} all-gather(f32[4,64,64,1]{2,1,3,0:T(8,128)S(1)} %copy.18), channel_id=5, replica_groups=mesh['gz'=4,'gx'=2,'gy'=4] {'gz'}, dimensions={0}, use_global_device_ids=true | all-gather | bytes 327680 | tf_op jit(solution)/shard_map/all_gather | solution.py:12
  86.1 6.0 %add_convert_fusion = bf16[4,64,64,128]{3,2,1,0:T(8,128)(2,1)S(1)} fusion(f32[4,64,64,128]{3,2,1,0:T(8,128)} %fusion.18, f32[4,64,64]{2,1,0:T(8,128)S(1)} %get-tuple-element.191, f32[4,128]{1,0:T(4,128)S(1)} %exp.25), kind=kLoop, calls=%fused_computation.38 | loop fusion | flops 6291456 | bytes 12650496 | tf_op jit(solution)/shard_map/convert_element_type | solution.py:116
  92.1 2.1 copy-done.1
  94.2 3.1 %collective-permute-start = (bf16[4,3,64,128]{3,2,1,0:T(8,128)(2,1)S(1)}, bf16[4,3,64,128]{3,2,1,0:T(8,128)(2,1)S(1)}, u32[]{:S(2)}, u32[]{:S(2)}) collective-permute-start(bf16[4,3,64,128]{3,2,1,0:T(8,128)(2,1)S(1)} %get-tuple-element.295), channel_id=1, source_target_pairs={{0,4},{1,5},{2,6},{3,7},{8,12},{9,13},{10,14},{11,15},{16,20},{17,... | collective-permute-start | bytes 589832 | tf_op jit(solution)/shard_map/ppermute | solution.py:34
  97.3 1.3 collective-permute-start.1
  99.2 1.5 fusion.9
  101.4 45.9 %psum.7 = f32[4]{0:T(128)S(1)} all-reduce(f32[4]{0:T(128)S(1)} %fusion.9), channel_id=1, replica_groups=mesh['gz'=4,'gx'=2,'gy'=4] {'gz','gx','gy'}, use_global_device_ids=true, to_apply=%region_10.11 | all-reduce | flops 4 | bytes 32 | tf_op jit(solution)/shard_map/psum | solution.py:126
  148.2 1.5 pad_maximum_fusion.2
  149.7 5.3 %collective-permute-start.2 = (bf16[4,70,3,128]{3,2,1,0:T(4,128)(2,1)S(1)}, bf16[4,70,3,128]{3,2,1,0:T(4,128)(2,1)S(1)}, u32[]{:S(2)}, u32[]{:S(2)}) collective-permute-start(bf16[4,70,3,128]{3,2,1,0:T(4,128)(2,1)S(1)} %get-tuple-element.292), channel_id=1, source_target_pairs={{0,1},{1,2},{2,3},{4,5},{5,6},{6,7},{8,9},{9,10},{10,11},{12,13},{... | collective-permute-start | bytes 645128 | tf_op jit(solution)/shard_map/ppermute | solution.py:34
  155.0 2.1 collective-permute-start.3
  158.5 4.4 %collective-permute-done.3 = bf16[4,70,3,128]{3,2,1,0:T(4,128)(2,1)S(1)} collective-permute-done((bf16[4,70,3,128]{3,2,1,0:T(4,128)(2,1)S(1)}, bf16[4,70,3,128]{3,2,1,0:T(4,128)(2,1)S(1)}, u32[]{:S(2)}, u32[]{:S(2)}) %collective-permute-start.3) | collective-permute-done | bytes 215072 | tf_op jit(solution)/shard_map/ppermute | solution.py:35
  162.9 8.4 %maximum_convert_fusion = f32[4,70,70,128]{3,2,1,0:T(8,128)} fusion(bf16[4,70,3,128]{3,2,1,0:T(4,128)(2,1)S(1)} %collective-permute-done.3, bf16[4,3,64,128]{3,2,1,0:T(8,128)(2,1)S(1)} %collective-permute-done.1, bf16[4,64,64,128]{3,2,1,0:T(8,128)(2,1)} %copy-done.1, bf16[4,3,64,128]{3,2,1,0:T(8,128)(2,1)S(1)} %collective-permute-done, ...), kind=kLoop, calls=%fused_computation.43 | loop fusion | flops 25088000 | bytes 15052800 | tf_op jit(solution)/shard_map/convert_element_type | solution.py:116
  171.3 30.3 %fusion.2 = f32[4,64,70,128]{3,2,1,0:T(8,128)} fusion(f32[4,70,70,128]{3,2,1,0:T(8,128)} %maximum_convert_fusion, f32[]{:T(128)} %bitcast.15, f32[]{:T(128)} %bitcast.14, f32[]{:T(128)} %bitcast.13, f32[]{:T(128)} %bitcast.12, f32[]{:T(128)} %bitcast.11, f32[]{:T(128)} %bitcast.10, f32[]{:T(128)} %bitcast), kind=kLoop, calls=%fused_computation.9 | loop fusion | flops 29818880 | bytes 73400352 | tf_op jit(solution)/shard_map/add | solution.py:52
  201.6 28.3 %fusion.21 = f32[64,64,128]{2,1,0:T(8,128)S(1)} fusion(f32[4,64,70,128]{3,2,1,0:T(8,128)} %fusion.2, f32[64,64,128]{2,1,0:T(8,128)S(1)} %get-tuple-element.294, f32[]{:T(128)} %bitcast.15, f32[]{:T(128)} %bitcast.14, f32[]{:T(128)} %bitcast.13, f32[]{:T(128)} %bitcast.12, f32[]{:T(128)} %bitcast.11, f32[]{:T(128)} %bitcast.10, f32[]{:T(128)} %bitcast, ...), kind=kLoop, calls=%fused_computation.42 | loop fusion | flops 33030144 | bytes 62914604 | tf_op jit(solution)/shard_map/reduce_sum | solution.py:123
  229.9 1.7 compare_select_fusion
  (59 shorter events, 8.7 us)
Async XLA Ops:
  15.8 4.5 %copy-start.2 = (bf16[4,64,64,128]{3,2,1,0:T(8,128)(2,1)S(1)}, bf16[4,64,64,128]{3,2,1,0:T(8,128)(2,1)}, u32[]{:S(2)}) copy-start(bf16[4,64,64,128]{3,2,1,0:T(8,128)(2,1)} %param.12) | copy-start | bytes 12582916
  28.9 3.2 %copy-start = (f32[4,64,64,128]{3,2,1,0:T(8,128)}, f32[4,64,64,128]{3,2,1,0:T(8,128)S(1)}, u32[]{:S(2)}) copy-start(f32[4,64,64,128]{3,2,1,0:T(8,128)S(1)} %fusion.8) | copy-start | bytes 25165828
  86.0 13.2 %copy-start.3 = (bf16[4,64,64,128]{3,2,1,0:T(8,128)(2,1)S(1)}, bf16[4,64,64,128]{3,2,1,0:T(8,128)(2,1)}, u32[]{:S(2)}) copy-start(bf16[4,64,64,128]{3,2,1,0:T(8,128)(2,1)} %param.12) | copy-start | bytes 12582916
  86.0 13.2 %copy-start.5 = (f32[64,64,128]{2,1,0:T(8,128)S(1)}, f32[64,64,128]{2,1,0:T(8,128)}, u32[]{:S(2)}) copy-start(f32[64,64,128]{2,1,0:T(8,128)} %get-tuple-element.291) | copy-start | bytes 6291460
  86.1 62.0 %copy-start.6 = (f32[16]{0:T(128)S(1)}, f32[16]{0:T(128)}, u32[]{:S(2)}) copy-start(f32[16]{0:T(128)} %param.15) | copy-start | bytes 196
  86.1 61.9 %copy-start.7 = (s32[4]{0:T(128)S(1)}, s32[4]{0:T(128)}, u32[]{:S(2)}) copy-start(s32[4]{0:T(128)} %param.14) | copy-start | bytes 52
  92.0 2.1 copy-start.1
  94.2 54.0 %collective-permute-start = (bf16[4,3,64,128]{3,2,1,0:T(8,128)(2,1)S(1)}, bf16[4,3,64,128]{3,2,1,0:T(8,128)(2,1)S(1)}, u32[]{:S(2)}, u32[]{:S(2)}) collective-permute-start(bf16[4,3,64,128]{3,2,1,0:T(8,128)(2,1)S(1)} %get-tuple-element.295), channel_id=1, source_target_pairs={{0,4},{1,5},{2,6},{3,7},{8,12},{9,13},{10,14},{11,15},{16,20},{17,... | collective-permute-start | bytes 589832 | tf_op jit(solution)/shard_map/ppermute | solution.py:34
  97.3 50.9 %collective-permute-start.1 = (bf16[4,3,64,128]{3,2,1,0:T(8,128)(2,1)S(1)}, bf16[4,3,64,128]{3,2,1,0:T(8,128)(2,1)S(1)}, u32[]{:S(2)}, u32[]{:S(2)}) collective-permute-start(bf16[4,3,64,128]{3,2,1,0:T(8,128)(2,1)S(1)} %get-tuple-element.296), channel_id=1, source_target_pairs={{4,0},{5,1},{6,2},{7,3},{12,8},{13,9},{14,10},{15,11},{20,16},{21,... | collective-permute-start | bytes 589832 | tf_op jit(solution)/shard_map/ppermute | solution.py:35
  149.7 8.8 %collective-permute-start.2 = (bf16[4,70,3,128]{3,2,1,0:T(4,128)(2,1)S(1)}, bf16[4,70,3,128]{3,2,1,0:T(4,128)(2,1)S(1)}, u32[]{:S(2)}, u32[]{:S(2)}) collective-permute-start(bf16[4,70,3,128]{3,2,1,0:T(4,128)(2,1)S(1)} %get-tuple-element.292), channel_id=1, source_target_pairs={{0,1},{1,2},{2,3},{4,5},{5,6},{6,7},{8,9},{9,10},{10,11},{12,13},{... | collective-permute-start | bytes 645128 | tf_op jit(solution)/shard_map/ppermute | solution.py:34
  155.0 8.0 %collective-permute-start.3 = (bf16[4,70,3,128]{3,2,1,0:T(4,128)(2,1)S(1)}, bf16[4,70,3,128]{3,2,1,0:T(4,128)(2,1)S(1)}, u32[]{:S(2)}, u32[]{:S(2)}) collective-permute-start(bf16[4,70,3,128]{3,2,1,0:T(4,128)(2,1)S(1)} %get-tuple-element.293), channel_id=1, source_target_pairs={{1,0},{2,1},{3,2},{5,4},{6,5},{7,6},{9,8},{10,9},{11,10},{13,12},{... | collective-permute-start | bytes 645128 | tf_op jit(solution)/shard_map/ppermute | solution.py:35
  201.6 28.3 %copy-start.4 = (s32[64,64,128]{2,1,0:T(8,128)S(1)}, s32[64,64,128]{2,1,0:T(8,128)}, u32[]{:S(2)}) copy-start(s32[64,64,128]{2,1,0:T(8,128)} %param.11) | copy-start | bytes 6291460
where the time goes:
time: 232 us
  other arithmetic  86 us (37%)
  blocking collectives  82.4 us (36%)
  local copies, waits for them, and re-layouts  24.7 us (11%)
  matrix products  19.7 us (8%)
  starting transfers between devices  11.8 us (5%)
  waiting for transfers between devices  5.3 us (2%)
    psum x1, blocking collectives, shards(): totals = lax.psum(partial_sums, ('gz', 'gx', 'gy'))  45.9 us
    add x1, other arithmetic, planar_filter(): along_x = along_x + taps[offset] * padded[:, offset:offset + width_x]  30.3 us
    reduce_sum x1, other arithmetic, shards(): combined = jnp.sum(weights[:, None, None, None] * filtered, axis=0)  28.3 us
    all_gather x2, blocking collectives, entering_2(): pieces = jax.tree.map(lambda part: lax.all_gather(part, axis), value)  25.8 us
    dot_general x1, matrix products, slab_smooth(): jnp.einsum('cxyj,cij->cxyi', forward, backward_map, precision=lax.Precisi...  11.1 us
    slice x2, local copies, waits for them, and re-layouts, slab_smooth(): local_forward[..., -1]  10.8 us
    unnamed x1, blocking collectives  10.7 us
    dot_general x1, matrix products, slab_smooth(): jnp.einsum('cxyj,cij->cxyi', field, forward_map, precision=lax.Precision....  8.58 us
  transfers between devices with their start and end apart: 4, of which 2 were waited for; matrix products, arithmetic and copies ran while one was open for 2% of the time, Pallas kernels for 0%

commit v1 on v0

--- a/solution.py
+++ b/solution.py
@@ -123,7 +123,7 @@
     combined = jnp.sum(weights[:, None, None, None] * filtered, axis=0)
     sensitivity = jnp.where(design_mask == 0, combined, 0.0).astype(jnp.float32)
     partial_sums = jnp.sum((dense**3)[None] * energy_wide, axis=(1, 2, 3))
-    totals = lax.psum(partial_sums, ("gz", "gx", "gy"))
+    totals = lax.psum(lax.psum(partial_sums, ("gx", "gy")), "gz")
     all_cells = (
         density.shape[0]
         * density.shape[1]

time: 232 us -> 203 us (0.88)
  blocking collectives: 82.4 us -> 48.5 us
  starting transfers between devices: 11.8 us -> 17.8 us
  other arithmetic: 86 us -> 82.5 us
  waiting for transfers between devices: 5.3 us -> 8.48 us
  local copies, waits for them, and re-layouts: 24.7 us -> 22.1 us
    psum x1, blocking collectives: 45.9 us -> 12.5 us  [shards(): totals = lax.psum(lax.psum(partial_sums, ('gx', 'gy')), 'gz')]
    ppermute x2, starting transfers between devices: 8.39 us -> 14.5 us  [with_halo(): before = lax.ppermute(last, axis, up)]
    ppermute x2, waiting for transfers between devices: 4.4 us -> 7.36 us  [with_halo(): after = lax.ppermute(initial, axis, down)]
    unnamed x21 -> x19, local copies, waits for them, and re-layouts: 7 us -> 4.34 us
  transfers between devices with their start and end apart: 4 -> 4, of which waited for: 2 -> 3; matrix products, arithmetic and copies ran while one was open for 2% -> 1% of each run, Pallas kernels for 0% -> 0%
where the time goes in v1:
time: 203 us
  other arithmetic  82.5 us (41%)
  blocking collectives  48.5 us (24%)
  local copies, waits for them, and re-layouts  22.1 us (11%)
  matrix products  21.9 us (11%)
  starting transfers between devices  17.8 us (9%)
  waiting for transfers between devices  8.48 us (4%)
    add x1, other arithmetic, planar_filter(): along_x = along_x + taps[offset] * padded[:, offset:offset + width_x]  30.4 us
    reduce_sum x1, other arithmetic, shards(): combined = jnp.sum(weights[:, None, None, None] * filtered, axis=0)  28.3 us
    all_gather x2, blocking collectives, entering_2(): pieces = jax.tree.map(lambda part: lax.all_gather(part, axis), value)  25.8 us
    ppermute x2, starting transfers between devices, with_halo(): before = lax.ppermute(last, axis, up)  14.5 us
    psum x1, blocking collectives, shards(): totals = lax.psum(lax.psum(partial_sums, ('gx', 'gy')), 'gz')  12.5 us
    dot_general x1, matrix products, slab_smooth(): jnp.einsum('cxyj,cij->cxyi', forward, backward_map, precision=lax.Precisi...  11.1 us
    slice x2, local copies, waits for them, and re-layouts, slab_smooth(): local_forward[..., -1]  10.8 us
    dot_general x1, matrix products, slab_smooth(): jnp.einsum('cxyj,cij->cxyi', field, forward_map, precision=lax.Precision....  10.8 us
  transfers between devices with their start and end apart: 4, of which 3 were waited for; matrix products, arithmetic and copies ran while one was open for 1% of the time, Pallas kernels for 0%

profile of v1, /device:TPU:1, one launch (start us, length us, event | category | flops | bytes accessed | tf_op | source)
XLA Modules:
  0.0 202.8 jit_solution(7798142580830456169)
XLA Ops:
  2.6 4.5 %broadcast_multiply_fusion = (f32[64,64,128]{2,1,0:T(8,128)S(1)}, f32[64,64,128]{2,1,0:T(8,128)S(1)}, f32[64,64,128]{2,1,0:T(8,128)}) fusion(f32[64,64,128]{2,1,0:T(8,128)} %param.10, s32[64,64,128]{2,1,0:T(8,128)} %param.11), kind=kLoop, calls=%fused_computation.51 | loop fusion | flops 4194304 | bytes 10485760 | tf_op jit(solution)/shard_map/mul | solution.py:114
  7.0 1.5 fusion.9
  8.5 12.5 %psum.14 = f32[4]{0:T(128)S(1)} all-reduce(f32[4]{0:T(128)S(1)} %fusion.9), channel_id=1, replica_groups=mesh['gz'=4,'gx'=2,'gy'=4] {'gx','gy'}, use_global_device_ids=true, to_apply=%region_10.11 | all-reduce | flops 4 | bytes 32 | tf_op jit(solution)/shard_map/psum | solution.py:126
  22.9 10.2 %all-reduce.2 = (f32[16]{0:T(128)S(1)}, f32[16]{0:T(128)S(1)}, f32[4]{0:T(128)S(1)}) all-reduce(f32[16]{0:T(128)S(1)} %dynamic-update-slice, f32[16]{0:T(128)S(1)} %dynamic-update-slice.1, f32[4]{0:T(128)S(1)} %psum.14), channel_id=2, replica_groups=mesh['gz'=4,'gx'=2,'gy'=4] {'gz'}, use_global_device_ids=true, to_apply=%add | all-reduce | flops 36 | bytes 288
  33.2 10.8 %fusion.8 = f32[4,64,64,128]{3,2,1,0:T(8,128)S(1)} fusion(bf16[4,64,64,128]{3,2,1,0:T(8,128)(2,1)} %param.12, f32[64,64,128]{2,1,0:T(8,128)S(1)} %get-tuple-element.291, f32[4,128]{1,0:T(4,128)S(1)} %get-tuple-element.299, f32[4,128]{1,0:T(4,128)S(1)} %reduce_window_sum.17, pred[128,128]{1,0:T(8,128)(4,1)S(1)} %iota_compare_fusion.1), kind=kOutput, calls=%fused_computation.21 | convolution fusion | flops 3225681920 | bytes 14700544 | tf_op jit(solution)/shard_map/cxyj,cij->cxyi/dot_general | solution.py:78
  44.0 3.2 %copy-done = f32[4,64,64,128]{3,2,1,0:T(8,128)} copy-done((f32[4,64,64,128]{3,2,1,0:T(8,128)}, f32[4,64,64,128]{3,2,1,0:T(8,128)S(1)}, u32[]{:S(2)}) %copy-start) | copy-done | bytes 8388632
  47.2 5.4 %slice.123 = f32[4,64,64,1]{3,2,1,0:T(8,128)} slice(f32[4,64,64,128]{3,2,1,0:T(8,128)S(1)} %fusion.8), slice={[0:4], [0:64], [0:64], [127:128]} | slice | bytes 131072 | tf_op jit(solution)/shard_map/slice | solution.py:85
  52.6 5.4 %copy.16 = f32[4,64,64,1]{2,1,3,0:T(8,128)S(1)} copy(f32[4,64,64,1]{3,2,1,0:T(8,128)} %slice.123) | data formatting | bytes 131072 | tf_op jit(solution)/shard_map/slice | solution.py:85
  58.0 13.6 %all-gather.1 = f32[16,64,64,1]{2,1,3,0:T(8,128)S(1)} all-gather(f32[4,64,64,1]{2,1,3,0:T(8,128)S(1)} %copy.16), channel_id=3, replica_groups=mesh['gz'=4,'gx'=2,'gy'=4] {'gz'}, dimensions={0}, use_global_device_ids=true | all-gather | bytes 327680 | tf_op jit(solution)/shard_map/all_gather | solution.py:12
  71.9 11.1 %fusion.18 = f32[4,64,64,128]{3,2,1,0:T(8,128)} fusion(f32[4,64,64,128]{3,2,1,0:T(8,128)} %copy-done, f32[4,64,64]{2,1,0:T(8,128)S(1)} %get-tuple-element.190, f32[4,128]{1,0:T(4,128)S(1)} %exp.23, f32[4,128]{1,0:T(4,128)S(1)} %rev.13, f32[4,128]{1,0:T(4,128)S(1)} %get-tuple-element.299, pred[128,128]{1,0:T(8,128)(4,1)S(1)} %iota_compare_fusion), kind=kOutput, calls=%fused_computation.39 | convolution fusion | flops 3225681920 | bytes 16865280 | tf_op jit(solution)/shard_map/cxyj,cij->cxyi/dot_general | solution.py:97
  83.0 5.4 %copy.18 = f32[4,64,64,1]{2,1,3,0:T(8,128)S(1)} copy(f32[4,64,64,1]{3,2,1,0:T(8,128)} %bitcast.43) | data formatting | bytes 131072 | tf_op jit(solution)/shard_map/slice | solution.py:102
  88.4 12.2 %all-gather.3 = f32[16,64,64,1]{2,1,3,0:T(8,128)S(1)} all-gather(f32[4,64,64,1]{2,1,3,0:T(8,128)S(1)} %copy.18), channel_id=5, replica_groups=mesh['gz'=4,'gx'=2,'gy'=4] {'gz'}, dimensions={0}, use_global_device_ids=true | all-gather | bytes 327680 | tf_op jit(solution)/shard_map/all_gather | solution.py:12
  101.1 5.2 %add_convert_fusion = bf16[4,64,64,128]{3,2,1,0:T(8,128)(2,1)S(1)} fusion(f32[4,64,64,128]{3,2,1,0:T(8,128)} %fusion.18, f32[4,64,64]{2,1,0:T(8,128)S(1)} %get-tuple-element.191, f32[4,128]{1,0:T(4,128)S(1)} %exp.25), kind=kLoop, calls=%fused_computation.38 | loop fusion | flops 6291456 | bytes 12650496 | tf_op jit(solution)/shard_map/convert_element_type | solution.py:116
  106.4 4.1 %collective-permute-start = (bf16[4,3,64,128]{3,2,1,0:T(8,128)(2,1)S(1)}, bf16[4,3,64,128]{3,2,1,0:T(8,128)(2,1)S(1)}, u32[]{:S(2)}, u32[]{:S(2)}) collective-permute-start(bf16[4,3,64,128]{3,2,1,0:T(8,128)(2,1)S(1)} %get-tuple-element.296), channel_id=1, source_target_pairs={{0,4},{1,5},{2,6},{3,7},{8,12},{9,13},{10,14},{11,15},{16,20},{17,... | collective-permute-start | bytes 589832 | tf_op jit(solution)/shard_map/ppermute | solution.py:34
  110.5 1.3 collective-permute-start.1
  113.9 3.0 %collective-permute-done.1 = bf16[4,3,64,128]{3,2,1,0:T(8,128)(2,1)S(1)} collective-permute-done((bf16[4,3,64,128]{3,2,1,0:T(8,128)(2,1)S(1)}, bf16[4,3,64,128]{3,2,1,0:T(8,128)(2,1)S(1)}, u32[]{:S(2)}, u32[]{:S(2)}) %collective-permute-start.1) | collective-permute-done | bytes 196640 | tf_op jit(solution)/shard_map/ppermute | solution.py:35
  117.1 10.5 %collective-permute-start.2 = (bf16[4,70,3,128]{3,2,1,0:T(4,128)(2,1)S(1)}, bf16[4,70,3,128]{3,2,1,0:T(4,128)(2,1)S(1)}, u32[]{:S(2)}, u32[]{:S(2)}) collective-permute-start(bf16[4,70,3,128]{3,2,1,0:T(4,128)(2,1)S(1)} %get-tuple-element.293), channel_id=1, source_target_pairs={{0,1},{1,2},{2,3},{4,5},{5,6},{6,7},{8,9},{9,10},{10,11},{12,13},{... | collective-permute-start | bytes 645128 | tf_op jit(solution)/shard_map/ppermute | solution.py:34
  127.6 1.9 collective-permute-start.3
  130.0 1.1 collective-permute-done.2
  131.2 4.4 %collective-permute-done.3 = bf16[4,70,3,128]{3,2,1,0:T(4,128)(2,1)S(1)} collective-permute-done((bf16[4,70,3,128]{3,2,1,0:T(4,128)(2,1)S(1)}, bf16[4,70,3,128]{3,2,1,0:T(4,128)(2,1)S(1)}, u32[]{:S(2)}, u32[]{:S(2)}) %collective-permute-start.3) | collective-permute-done | bytes 215072 | tf_op jit(solution)/shard_map/ppermute | solution.py:35
  135.5 6.8 %maximum_convert_fusion = f32[4,70,70,128]{3,2,1,0:T(8,128)} fusion(bf16[4,70,3,128]{3,2,1,0:T(4,128)(2,1)S(1)} %collective-permute-done.3, bf16[4,3,64,128]{3,2,1,0:T(8,128)(2,1)S(1)} %collective-permute-done.1, bf16[4,64,64,128]{3,2,1,0:T(8,128)(2,1)S(1)} %add_convert_fusion, bf16[4,3,64,128]{3,2,1,0:T(8,128)(2,1)S(1)} %collective-permute-done, ...), kind=kLoop, calls=%fused_computation.43 | loop fusion | flops 25088000 | bytes 15052800 | tf_op jit(solution)/shard_map/convert_element_type | solution.py:116
  142.4 30.4 %fusion.2 = f32[4,64,70,128]{3,2,1,0:T(8,128)} fusion(f32[4,70,70,128]{3,2,1,0:T(8,128)} %maximum_convert_fusion, f32[]{:T(128)} %bitcast.15, f32[]{:T(128)} %bitcast.14, f32[]{:T(128)} %bitcast.13, f32[]{:T(128)} %bitcast.12, f32[]{:T(128)} %bitcast.11, f32[]{:T(128)} %bitcast.10, f32[]{:T(128)} %bitcast), kind=kLoop, calls=%fused_computation.9 | loop fusion | flops 29818880 | bytes 73400352 | tf_op jit(solution)/shard_map/add | solution.py:52
  172.8 28.3 %fusion.21 = f32[64,64,128]{2,1,0:T(8,128)S(1)} fusion(f32[4,64,70,128]{3,2,1,0:T(8,128)} %fusion.2, f32[64,64,128]{2,1,0:T(8,128)S(1)} %copy-done.3, f32[]{:T(128)} %bitcast.15, f32[]{:T(128)} %bitcast.14, f32[]{:T(128)} %bitcast.13, f32[]{:T(128)} %bitcast.12, f32[]{:T(128)} %bitcast.11, f32[]{:T(128)} %bitcast.10, f32[]{:T(128)} %bitcast, ...), kind=kLoop, calls=%fused_computation.42 | loop fusion | flops 33030144 | bytes 62914604 | tf_op jit(solution)/shard_map/reduce_sum | solution.py:123
  201.1 1.7 compare_select_fusion
  (57 shorter events, 7.4 us)
Async XLA Ops:
  2.5 4.5 %copy-start.1 = (bf16[4,64,64,128]{3,2,1,0:T(8,128)(2,1)S(1)}, bf16[4,64,64,128]{3,2,1,0:T(8,128)(2,1)}, u32[]{:S(2)}) copy-start(bf16[4,64,64,128]{3,2,1,0:T(8,128)(2,1)} %param.12) | copy-start | bytes 12582916
  2.5 18.6 %copy-start.6 = (u32[32]{0:T(128)S(1)}, u32[32]{0:T(128)}, u32[]{:S(2)}) copy-start(u32[32]{0:T(128)} %constant.87) | copy-start | bytes 388
  43.9 3.2 %copy-start = (f32[4,64,64,128]{3,2,1,0:T(8,128)}, f32[4,64,64,128]{3,2,1,0:T(8,128)S(1)}, u32[]{:S(2)}) copy-start(f32[4,64,64,128]{3,2,1,0:T(8,128)S(1)} %fusion.8) | copy-start | bytes 25165828
  100.6 13.1 %copy-start.4 = (f32[16]{0:T(128)S(1)}, f32[16]{0:T(128)}, u32[]{:S(2)}) copy-start(f32[16]{0:T(128)} %param.15) | copy-start | bytes 196
  100.6 13.1 %copy-start.5 = (s32[4]{0:T(128)S(1)}, s32[4]{0:T(128)}, u32[]{:S(2)}) copy-start(s32[4]{0:T(128)} %param.14) | copy-start | bytes 52
  106.4 7.5 %collective-permute-start = (bf16[4,3,64,128]{3,2,1,0:T(8,128)(2,1)S(1)}, bf16[4,3,64,128]{3,2,1,0:T(8,128)(2,1)S(1)}, u32[]{:S(2)}, u32[]{:S(2)}) collective-permute-start(bf16[4,3,64,128]{3,2,1,0:T(8,128)(2,1)S(1)} %get-tuple-element.296), channel_id=1, source_target_pairs={{0,4},{1,5},{2,6},{3,7},{8,12},{9,13},{10,14},{11,15},{16,20},{17,... | collective-permute-start | bytes 589832 | tf_op jit(solution)/shard_map/ppermute | solution.py:34
  110.5 6.4 %collective-permute-start.1 = (bf16[4,3,64,128]{3,2,1,0:T(8,128)(2,1)S(1)}, bf16[4,3,64,128]{3,2,1,0:T(8,128)(2,1)S(1)}, u32[]{:S(2)}, u32[]{:S(2)}) collective-permute-start(bf16[4,3,64,128]{3,2,1,0:T(8,128)(2,1)S(1)} %get-tuple-element.297), channel_id=1, source_target_pairs={{4,0},{5,1},{6,2},{7,3},{12,8},{13,9},{14,10},{15,11},{20,16},{21,... | collective-permute-start | bytes 589832 | tf_op jit(solution)/shard_map/ppermute | solution.py:35
  117.1 14.0 %collective-permute-start.2 = (bf16[4,70,3,128]{3,2,1,0:T(4,128)(2,1)S(1)}, bf16[4,70,3,128]{3,2,1,0:T(4,128)(2,1)S(1)}, u32[]{:S(2)}, u32[]{:S(2)}) collective-permute-start(bf16[4,70,3,128]{3,2,1,0:T(4,128)(2,1)S(1)} %get-tuple-element.293), channel_id=1, source_target_pairs={{0,1},{1,2},{2,3},{4,5},{5,6},{6,7},{8,9},{9,10},{10,11},{12,13},{... | collective-permute-start | bytes 645128 | tf_op jit(solution)/shard_map/ppermute | solution.py:34
  127.6 8.0 %collective-permute-start.3 = (bf16[4,70,3,128]{3,2,1,0:T(4,128)(2,1)S(1)}, bf16[4,70,3,128]{3,2,1,0:T(4,128)(2,1)S(1)}, u32[]{:S(2)}, u32[]{:S(2)}) collective-permute-start(bf16[4,70,3,128]{3,2,1,0:T(4,128)(2,1)S(1)} %get-tuple-element.294), channel_id=1, source_target_pairs={{1,0},{2,1},{3,2},{5,4},{6,5},{7,6},{9,8},{10,9},{11,10},{13,12},{... | collective-permute-start | bytes 645128 | tf_op jit(solution)/shard_map/ppermute | solution.py:35
  142.4 30.4 %copy-start.3 = (f32[64,64,128]{2,1,0:T(8,128)S(1)}, f32[64,64,128]{2,1,0:T(8,128)}, u32[]{:S(2)}) copy-start(f32[64,64,128]{2,1,0:T(8,128)} %get-tuple-element.295) | copy-start | bytes 6291460
  172.8 28.3 %copy-start.2 = (s32[64,64,128]{2,1,0:T(8,128)S(1)}, s32[64,64,128]{2,1,0:T(8,128)}, u32[]{:S(2)}) copy-start(s32[64,64,128]{2,1,0:T(8,128)} %param.11) | copy-start | bytes 6291460
